TPU v7x, 32 devices: a whole 2x2x4 slice. The times are simulated.
32 devices in a mesh: section: 2 (over core), ctx: 4 (over y, x), tp: 4 (over z).
Axes of the slice: x: 2, y: 2, z: 4, core: 2. Of those that a mesh axis runs over, the one named last changes fastest.
Arguments:
- inputs: bfloat16 [4, 1024, 2048], P(None, ('ctx', 'tp')), may hold values from -6 to 6
- segments: int32 [4, 1024], replicated, may hold values from 0 to 3, never falling along the last dimension, each value on 1 to 512 neighbouring positions
- cotangent: bfloat16 [4, 1024, 2048], P(None, ('ctx', 'tp')), may hold values from -6 to 6
- ln_gain: bfloat16 [2, 2048], P('section'), may hold values from 0.5 to 1.5
- ln_bias: bfloat16 [2, 2048], P('section'), may hold values from -3 to 3
- qkv_weight: bfloat16 [2, 3, 2048, 2048], P('section', None, None, 'tp'), may hold values from -1 to 1, as said below
- qkv_bias: bfloat16 [2, 3, 2048], P('section', None, 'tp'), may hold values from -3 to 3
- dense_weight: bfloat16 [2, 2048, 2048], P('section', 'tp'), may hold values from -0.75 to 0.75
- fc1_weight: bfloat16 [2, 2048, 8192], P('section', None, 'tp'), may hold values from -0.125 to 0.125
- fc1_bias: bfloat16 [2, 8192], P('section', 'tp'), may hold values from -3 to 3
- fc2_weight: bfloat16 [2, 8192, 2048], P('section', 'tp'), may hold values from -0.0625 to 0.0625
- out_bias: bfloat16 [2, 2048], P('section'), may hold values from -3 to 3
Outputs:
- layer_outputs: bfloat16 [2, 4, 1024, 2048], P('section', None, ('ctx', 'tp'))
- input_grads: bfloat16 [2, 4, 1024, 2048], P('section', None, ('ctx', 'tp'))
- ln_gain_grad: float32 [2, 2048], P('section')
- ln_bias_grad: float32 [2, 2048], P('section')
- qkv_weight_grad: float32 [2, 3, 2048, 2048], P('section', None, None, 'tp')
- qkv_bias_grad: float32 [2, 3, 2048], P('section', None, 'tp')
- dense_weight_grad: float32 [2, 2048, 2048], P('section', 'tp')
- fc1_weight_grad: float32 [2, 2048, 8192], P('section', None, 'tp')
- fc1_bias_grad: float32 [2, 8192], P('section', 'tp')
- fc2_weight_grad: float32 [2, 8192, 2048], P('section', 'tp')
- out_bias_grad: float32 [2, 2048], P('section')
Inputs may be any that keep to these rules, and one draw needn't show every extreme that they name: `segments`: within a sequence the ids never fall; each of the 4 documents has 1 to 512 tokens, one exactly 512. `qkv_weight`: entries of order 2048^(-1/2).
All inputs are finite; a program needn't handle non-finite values.
Results may differ from a plain program's by a relative error of at most 0.02.
Values may be sent and summed in bfloat16 or wider, within the bound.
No kernel may reach another device: no remote copies, remote signals or barrier semaphores. Data moves between devices by JAX's collectives and lax.ppermute only.
A program may use at most 640 MiB of HBM per device.

v0:
```python
import jax
import jax.numpy as jnp
from jax import lax
from jax.sharding import PartitionSpec as P

HEAD = 64
ROT = 32
EPSILON = 1e-05
NEGATIVE = -1e30
GELU_ROOT = 0.7978845608028654
GELU_CUBE = 0.044715


def from_behind(x, axis, by):
    length = lax.axis_size(axis)
    pairs = [(i, i + by) for i in range(length) if 0 <= i + by < length]
    return lax.ppermute(x, axis, pairs)


def rope_tables(positions, rot_dims):
    half_dims = rot_dims // 2
    frequency = 10000.0 ** (-(2.0 * jnp.arange(half_dims, dtype=jnp.float32)) / rot_dims)
    angles = positions.astype(jnp.float32)[:, None] * frequency[None, :]
    return (jnp.cos(angles)[:, None, :], jnp.sin(angles)[:, None, :])


def rotate(values_in, cosine, sine, rot_dims):
    half_dims = rot_dims // 2
    lower_half = values_in[..., :half_dims]
    upper_half = values_in[..., half_dims:rot_dims]
    return jnp.concatenate(
        [
            lower_half * cosine - upper_half * sine,
            upper_half * cosine + lower_half * sine,
            values_in[..., rot_dims:],
        ],
        axis=-1,
    )


def unrotate(grads_in, cosine, sine, rot_dims):
    half_dims = rot_dims // 2
    lower_half = grads_in[..., :half_dims]
    upper_half = grads_in[..., half_dims:rot_dims]
    return jnp.concatenate(
        [
            lower_half * cosine + upper_half * sine,
            upper_half * cosine - lower_half * sine,
            grads_in[..., rot_dims:],
        ],
        axis=-1,
    )


def gelu_slope(pre_act):
    tangent = jnp.tanh(GELU_ROOT * (pre_act + GELU_CUBE * pre_act * pre_act * pre_act))
    return 0.5 * (1.0 + tangent) + 0.5 * pre_act * (1.0 - tangent * tangent) * GELU_ROOT * (
        1.0 + 3.0 * GELU_CUBE * pre_act * pre_act
    )


def normalize(x_rows):
    centered = x_rows - jnp.mean(x_rows, axis=1, keepdims=True)
    inv_std = lax.rsqrt(jnp.mean(centered * centered, axis=1, keepdims=True) + EPSILON)
    return (centered * inv_std, inv_std)


def take_slot(buffer, slot_index):
    return lax.dynamic_index_in_dim(buffer, slot_index, 0, keepdims=False)


def put_slot(buffer, slot_index, leaf_value, active):
    return lax.dynamic_update_index_in_dim(
        buffer, jnp.where(active, leaf_value, take_slot(buffer, slot_index)), slot_index, 0
    )


def on_device(
    inputs,
    segments,
    cotangent,
    ln_gain,
    ln_bias,
    qkv_weight,
    qkv_bias,
    dense_weight,
    fc1_weight,
    fc1_bias,
    fc2_weight,
    out_bias,
):
    sections = lax.axis_size("section")
    section_id = lax.axis_index("section")
    ctx_id = lax.axis_index("ctx")
    batches, row_count, model_width = inputs.shape
    ctx_rows = row_count * lax.axis_size("tp")
    total_rows = ctx_rows * lax.axis_size("ctx")
    local_dim = qkv_weight.shape[3]
    heads_local = local_dim // HEAD
    score_scale = HEAD ** (-0.5)
    gain_vec = ln_gain[0].astype(jnp.float32)
    shift_vec = ln_bias[0].astype(jnp.float32)
    w_in = jnp.concatenate(
        [qkv_weight[0, 0], qkv_weight[0, 1], qkv_weight[0, 2], fc1_weight[0]], axis=1
    )
    bias_in = jnp.concatenate([qkv_bias[0].reshape(-1), fc1_bias[0]]).astype(jnp.float32)
    w_out = jnp.concatenate([dense_weight[0], fc2_weight[0]], axis=0)
    bias_vec = out_bias[0].astype(jnp.float32)
    query_pos = ctx_id * ctx_rows + jnp.arange(ctx_rows, dtype=jnp.int32)
    cosine, sine = rope_tables(query_pos, ROT)
    key_pos = jnp.arange(total_rows, dtype=jnp.int32)
    contract_rows = (((0,), (0,)), ((), ()))
    contract_cols = (((1,), (1,)), ((), ()))
    received = jnp.zeros((row_count, model_width), jnp.bfloat16)
    layer_out = jnp.zeros((batches, row_count, model_width), jnp.bfloat16)
    buffers = None
    for clock_tick in range(batches + sections - 1):
        micro_batch = clock_tick - section_id
        active = (micro_batch >= 0) & (micro_batch < batches)
        slot_index = jnp.clip(micro_batch, 0, batches - 1)
        x_rows = jnp.where(section_id == 0, take_slot(inputs, slot_index), received).astype(
            jnp.float32
        )
        doc_all = take_slot(segments, slot_index)
        normalized, inv_std = normalize(x_rows)
        normed_b = (normalized * gain_vec + shift_vec).astype(jnp.bfloat16)
        doc_rows = lax.dynamic_slice_in_dim(doc_all, ctx_id * ctx_rows, ctx_rows)
        stored = {}
        projected = jnp.dot(
            lax.all_gather(normed_b, "tp", axis=0, tiled=True),
            w_in,
            preferred_element_type=jnp.float32,
        )
        projected = projected + bias_in
        query_pre = projected[:, :local_dim].reshape(ctx_rows, heads_local, HEAD)
        key_pre = projected[:, local_dim : 2 * local_dim].reshape(ctx_rows, heads_local, HEAD)
        queries_b = rotate(query_pre, cosine, sine, ROT).astype(jnp.bfloat16)
        keys_b = rotate(key_pre, cosine, sine, ROT).astype(jnp.bfloat16)
        values_b = (
            projected[:, 2 * local_dim : 3 * local_dim]
            .reshape(ctx_rows, heads_local, HEAD)
            .astype(jnp.bfloat16)
        )
        up_pre = projected[:, 3 * local_dim :]
        run_max = jnp.full((heads_local, ctx_rows), NEGATIVE, jnp.float32)
        keys_part = lax.all_gather(keys_b, "ctx", axis=0, tiled=True)
        values_part = lax.all_gather(values_b, "ctx", axis=0, tiled=True)
        part_rows = keys_part.shape[0]
        part_pos = jnp.arange(part_rows, dtype=jnp.int32)
        allowed = (part_pos[None, :] <= query_pos[:, None]) & (
            doc_all[None, :] == doc_rows[:, None]
        )
        scores = (
            jnp.einsum("qhd,khd->hqk", queries_b, keys_part, preferred_element_type=jnp.float32)
            * score_scale
        )
        scores = jnp.where(allowed[None], scores, NEGATIVE)
        new_max = jnp.maximum(run_max, jnp.max(scores, axis=2))
        weights = jnp.where(allowed[None], jnp.exp(scores - new_max[:, :, None]), 0.0)
        run_sum = jnp.sum(weights, axis=2)
        accumulated = jnp.einsum(
            "hqk,khd->hqd",
            weights.astype(jnp.bfloat16),
            values_part,
            preferred_element_type=jnp.float32,
        )
        run_max, run_sum, accumulated = (new_max, run_sum, accumulated)
        attended = jnp.transpose(accumulated / run_sum[:, :, None], (1, 0, 2))
        log_total = run_max + jnp.log(run_sum)
        attended_b = attended.reshape(ctx_rows, local_dim).astype(jnp.bfloat16)
        gelu_b = jax.nn.gelu(up_pre, approximate=True).astype(jnp.bfloat16)
        branch_in = jnp.concatenate([attended_b, gelu_b], axis=1)
        branch = lax.psum_scatter(
            jnp.dot(branch_in, w_out, preferred_element_type=jnp.float32).astype(jnp.bfloat16),
            "tp",
            scatter_dimension=0,
            tiled=True,
        ).astype(jnp.float32)
        result = x_rows + branch + bias_vec
        stored["x_rows"] = x_rows.astype(jnp.bfloat16)
        stored["queries"] = queries_b
        stored["keys"] = keys_b
        stored["values"] = values_b
        stored["up_pre"] = up_pre
        stored["branch_in"] = branch_in
        stored["attended"] = attended
        stored["log_total"] = log_total
        result, stored = (result, stored)
        result_b = result.astype(jnp.bfloat16)
        if buffers is None:
            buffers = jax.tree.map(
                lambda leaf_value: jnp.zeros((batches,) + leaf_value.shape, leaf_value.dtype),
                stored,
            )
        buffers = jax.tree.map(
            lambda buffer, leaf_value: put_slot(buffer, slot_index, leaf_value, active),
            buffers,
            stored,
        )
        layer_out = put_slot(layer_out, slot_index, result_b, active)
        received = from_behind(result_b, "section", 1)
    received = jnp.zeros((row_count, model_width), jnp.bfloat16)
    grad_inputs = jnp.zeros((batches, row_count, model_width), jnp.bfloat16)
    totals = None
    for clock_tick in range(batches + sections - 1):
        micro_batch = clock_tick - (sections - 1 - section_id)
        active = (micro_batch >= 0) & (micro_batch < batches)
        slot_index = jnp.clip(micro_batch, 0, batches - 1)
        grad_out = jnp.where(
            section_id == sections - 1, take_slot(cotangent, slot_index), received
        ).astype(jnp.float32)
        stored = jax.tree.map(lambda buffer: take_slot(buffer, slot_index), buffers)
        doc_all = take_slot(segments, slot_index)
        backward_normalized, backward_inv_std = normalize(stored["x_rows"].astype(jnp.float32))
        backward_normed_b = (backward_normalized * gain_vec + shift_vec).astype(jnp.bfloat16)
        backward_doc_rows = lax.dynamic_slice_in_dim(doc_all, ctx_id * ctx_rows, ctx_rows)
        backward_branch_in = stored["branch_in"]
        grad_out_b = grad_out.astype(jnp.bfloat16)
        fold_pieces = lax.all_gather(grad_out_b, "tp", axis=0, tiled=True)
        grad_w = lax.dot_general(
            backward_branch_in, fold_pieces, contract_rows, preferred_element_type=jnp.float32
        )
        grad_rows = lax.dot_general(
            fold_pieces, w_out, contract_cols, preferred_element_type=jnp.float32
        )
        grad_attn_b = (
            grad_rows[:, :local_dim].astype(jnp.bfloat16).reshape(ctx_rows, heads_local, HEAD)
        )
        grad_up = grad_rows[:, local_dim:] * gelu_slope(stored["up_pre"])
        row_delta = jnp.transpose(
            jnp.sum(grad_attn_b.astype(jnp.float32) * stored["attended"], axis=2)
        )
        keys_all = lax.all_gather(stored["keys"], "ctx", axis=0, tiled=True)
        values_all = lax.all_gather(stored["values"], "ctx", axis=0, tiled=True)
        backward_queries_b = stored["queries"]
        backward_allowed = (key_pos[None, :] <= query_pos[:, None]) & (
            doc_all[None, :] == backward_doc_rows[:, None]
        )
        backward_scores = (
            jnp.einsum(
                "qhd,khd->hqk", backward_queries_b, keys_all, preferred_element_type=jnp.float32
            )
            * score_scale
        )
        probs = jnp.where(
            backward_allowed[None], jnp.exp(backward_scores - stored["log_total"][:, :, None]), 0.0
        )
        grad_probs = jnp.einsum(
            "qhd,khd->hqk", grad_attn_b, values_all, preferred_element_type=jnp.float32
        )
        grad_scores_b = (probs * (grad_probs - row_delta[:, :, None])).astype(jnp.bfloat16)
        grad_query = (
            jnp.einsum("hqk,khd->qhd", grad_scores_b, keys_all, preferred_element_type=jnp.float32)
            * score_scale
        )
        probs_b = probs.astype(jnp.bfloat16)
        grad_key_part = (
            jnp.einsum(
                "hqk,qhd->khd",
                grad_scores_b,
                backward_queries_b,
                preferred_element_type=jnp.float32,
            )
            * score_scale
        )
        grad_value_part = jnp.einsum(
            "hqk,qhd->khd", probs_b, grad_attn_b, preferred_element_type=jnp.float32
        )
        key_grads = (
            lax.psum_scatter(
                jnp.concatenate([grad_key_part, grad_value_part], axis=2)
                .reshape(ctx_rows * lax.axis_size("ctx"), 2 * local_dim)
                .astype(jnp.bfloat16),
                "ctx",
                scatter_dimension=0,
                tiled=True,
            )
            .astype(jnp.float32)
            .reshape(ctx_rows, heads_local, 2 * HEAD)
        )
        grad_key_raw = key_grads[..., :HEAD]
        grad_value = key_grads[..., HEAD:]
        grad_key = unrotate(grad_key_raw, cosine, sine, ROT)
        grad_query = unrotate(grad_query, cosine, sine, ROT)
        grad_proj_b = jnp.concatenate(
            [
                grad_query.reshape(ctx_rows, local_dim),
                grad_key.reshape(ctx_rows, local_dim),
                grad_value.reshape(ctx_rows, local_dim),
                grad_up,
            ],
            axis=1,
        ).astype(jnp.bfloat16)
        grad_bias_in = jnp.sum(grad_proj_b.astype(jnp.float32), axis=0)
        grad_w_in = lax.dot_general(
            lax.all_gather(backward_normed_b, "tp", axis=0, tiled=True),
            grad_proj_b,
            contract_rows,
            preferred_element_type=jnp.float32,
        )
        grad_normed = lax.psum_scatter(
            lax.dot_general(
                grad_proj_b, w_in, contract_cols, preferred_element_type=jnp.float32
            ).astype(jnp.bfloat16),
            "tp",
            scatter_dimension=0,
            tiled=True,
        ).astype(jnp.float32)
        grad_gain = jnp.sum(grad_normed * backward_normalized, axis=0)
        grad_shift = jnp.sum(grad_normed, axis=0)
        scaled = grad_normed * gain_vec
        grad_x = grad_out + backward_inv_std * (
            scaled
            - jnp.mean(scaled, axis=1, keepdims=True)
            - backward_normalized * jnp.mean(scaled * backward_normalized, axis=1, keepdims=True)
        )
        grad_x, terms = (
            grad_x,
            (grad_w_in, grad_w, grad_bias_in, grad_gain, grad_shift, jnp.sum(grad_out, axis=0)),
        )
        terms = tuple((jnp.where(active, term_value, 0.0) for term_value in terms))
        totals = terms if totals is None else jax.tree.map(jnp.add, totals, terms)
        grad_x_b = grad_x.astype(jnp.bfloat16)
        grad_inputs = put_slot(grad_inputs, slot_index, grad_x_b, active)
        received = from_behind(grad_x_b, "section", -1)
    total_w_in, total_w_out, total_bias_in, total_gain, total_shift, total_bias_out = totals
    sum_w_in, sum_w_out, sum_bias_in, sum_gain, sum_shift, sum_bias_out = (
        lax.psum(total_w_in.astype(jnp.bfloat16), "ctx").astype(jnp.float32),
        lax.psum(total_w_out.astype(jnp.bfloat16), "ctx").astype(jnp.float32),
        lax.psum(total_bias_in.astype(jnp.bfloat16), "ctx").astype(jnp.float32),
        lax.psum(total_gain.astype(jnp.bfloat16), "ctx").astype(jnp.float32),
        lax.psum(total_shift.astype(jnp.bfloat16), "ctx").astype(jnp.float32),
        lax.psum(total_bias_out.astype(jnp.bfloat16), "ctx").astype(jnp.float32),
    )
    sum_gain, sum_shift, sum_bias_out = lax.psum((sum_gain, sum_shift, sum_bias_out), "tp")
    qkv_grad = jnp.transpose(
        sum_w_in[:, : 3 * local_dim].reshape(model_width, 3, local_dim), (1, 0, 2)
    )
    return (
        layer_out[None],
        grad_inputs[None],
        sum_gain[None],
        sum_shift[None],
        qkv_grad[None],
        sum_bias_in[: 3 * local_dim].reshape(3, local_dim)[None],
        sum_w_out[:local_dim][None],
        sum_w_in[:, 3 * local_dim :][None],
        sum_bias_in[3 * local_dim :][None],
        sum_w_out[local_dim:][None],
        sum_bias_out[None],
    )


def solution(mesh):
    return jax.shard_map(
        on_device,
        mesh=mesh,
        in_specs=(
            P(None, ("ctx", "tp"), None),
            P(),
            P(None, ("ctx", "tp"), None),
            P("section", None),
            P("section", None),
            P("section", None, None, "tp"),
            P("section", None, "tp"),
            P("section", "tp", None),
            P("section", None, "tp"),
            P("section", "tp"),
            P("section", "tp", None),
            P("section", None),
        ),
        out_specs=(
            P("section", None, ("ctx", "tp"), None),
            P("section", None, ("ctx", "tp"), None),
            P("section", None),
            P("section", None),
            P("section", None, None, "tp"),
            P("section", None, "tp"),
            P("section", "tp", None),
            P("section", None, "tp"),
            P("section", "tp"),
            P("section", "tp", None),
            P("section", None),
        ),
        check_vma=False,
    )
```

profile of v0, /device:TPU:0, one launch (start us, length us, event | category | flops | bytes accessed | tf_op | source)
XLA Modules:
  0.0 2298.0 jit_solution(12967685389564836496)
XLA Ops:
  19.1 12.1 pad_maximum_fusion
  31.2 12.5 all-gather.47.cloned.1.call-done
  62.0 18.5 all-gather.49.cloned.1.call-done
  89.4 19.9 all-gather.51.cloned.1.call-done
  124.1 27.4 %reduce-scatter.16.cloned.1.call-done = bf16[64,2048]{1,0:T(8,128)(2,1)} async-done(((bf16[256,2048]{1,0:T(8,128)(2,1)}), bf16[64,2048]{1,0:T(8,128)(2,1)}) %reduce-scatter.16.cloned.1.call-update) | async-done | bytes 262160 | tf_op jit(solution)/shard_map/reduce_scatter | solution.py:173
  156.8 27.9 %all-gather.53.cloned.1.call-done = bf16[256,2048]{1,0:T(8,128)(2,1)} async-done(((bf16[64,2048]{1,0:T(8,128)(2,1)}), bf16[256,2048]{1,0:T(8,128)(2,1)}) %all-gather.53.cloned.1.call-update) | async-done | bytes 1048592 | tf_op jit(solution)/shard_map/all_gather | solution.py:130
  215.8 13.5 all-gather.55.cloned.1.call-done
  238.3 19.2 all-gather.57.cloned.1.call-done
  275.1 26.7 %reduce-scatter.18.cloned.1.call-done = bf16[64,2048]{1,0:T(8,128)(2,1)} async-done(((bf16[256,2048]{1,0:T(8,128)(2,1)}), bf16[64,2048]{1,0:T(8,128)(2,1)}) %reduce-scatter.18.cloned.1.call-update) | async-done | bytes 262160 | tf_op jit(solution)/shard_map/reduce_scatter | solution.py:173
  308.2 27.7 %all-gather.59.cloned.1.call-done = bf16[256,2048]{1,0:T(8,128)(2,1)} async-done(((bf16[64,2048]{1,0:T(8,128)(2,1)}), bf16[256,2048]{1,0:T(8,128)(2,1)}) %all-gather.59.cloned.1.call-update) | async-done | bytes 1048592 | tf_op jit(solution)/shard_map/all_gather | solution.py:130
  363.1 17.4 all-gather.61.cloned.1.call-done
  389.5 19.2 all-gather.63.cloned.1.call-done
  426.3 26.7 %reduce-scatter.20.cloned.1.call-done = bf16[64,2048]{1,0:T(8,128)(2,1)} async-done(((bf16[256,2048]{1,0:T(8,128)(2,1)}), bf16[64,2048]{1,0:T(8,128)(2,1)}) %reduce-scatter.20.cloned.1.call-update) | async-done | bytes 262160 | tf_op jit(solution)/shard_map/reduce_scatter | solution.py:173
  459.6 27.5 %all-gather.65.cloned.1.call-done = bf16[256,2048]{1,0:T(8,128)(2,1)} async-done(((bf16[64,2048]{1,0:T(8,128)(2,1)}), bf16[256,2048]{1,0:T(8,128)(2,1)}) %all-gather.65.cloned.1.call-update) | async-done | bytes 1048592 | tf_op jit(solution)/shard_map/all_gather | solution.py:130
  516.7 14.9 all-gather.67.cloned.1.call-done
  540.7 19.0 all-gather.69.cloned.1.call-done
  598.6 19.9 reduce-scatter.22.cloned.1.call-done
  732.7 20.9 all-gather.95.cloned.1.call-done
  762.5 19.2 all-gather.99.cloned.1.call-done
  853.4 26.6 %reduce-scatter.28.cloned.1.call-done = bf16[64,2048]{1,0:T(8,128)(2,1)} async-done(((bf16[256,2048]{1,0:T(8,128)(2,1)}), bf16[64,2048]{1,0:T(8,128)(2,1)}) %reduce-scatter.28.cloned.1.call-update) | async-done | bytes 262160 | tf_op jit(solution)/shard_map/reduce_scatter | solution.py:301
  892.1 14.6 all-gather.101.cloned.1.call-done
  912.8 23.4 %all-gather.77.cloned.1.call-done = bf16[256,2048]{1,0:T(8,128)(2,1)} async-done(((bf16[64,2048]{1,0:T(8,128)(2,1)}), bf16[256,2048]{1,0:T(8,128)(2,1)}) %all-gather.77.cloned.1.call-update) | async-done | bytes 1048592 | tf_op jit(solution)/shard_map/all_gather | solution.py:219
  983.3 25.3 %reduce-scatter.30.cloned.1.call-done = bf16[256,1024]{0,1:T(8,128)(2,1)} async-done(((bf16[1024,1024]{0,1:T(8,128)(2,1)}), bf16[256,1024]{0,1:T(8,128)(2,1)}) %reduce-scatter.30.cloned.1.call-update) | async-done | bytes 524304 | tf_op jit(solution)/shard_map/reduce_scatter | solution.py:270
  1036.9 25.0 %reduce-scatter.32.cloned.1.call-done = bf16[64,2048]{1,0:T(8,128)(2,1)} async-done(((bf16[256,2048]{1,0:T(8,128)(2,1)}), bf16[64,2048]{1,0:T(8,128)(2,1)}) %reduce-scatter.32.cloned.1.call-update) | async-done | bytes 262160 | tf_op jit(solution)/shard_map/reduce_scatter | solution.py:301
  1074.3 14.3 all-gather.105.cloned.1.call-done
  1094.5 23.6 %all-gather.79.cloned.1.call-done = bf16[256,2048]{1,0:T(8,128)(2,1)} async-done(((bf16[64,2048]{1,0:T(8,128)(2,1)}), bf16[256,2048]{1,0:T(8,128)(2,1)}) %all-gather.79.cloned.1.call-update) | async-done | bytes 1048592 | tf_op jit(solution)/shard_map/all_gather | solution.py:219
  1165.6 25.3 %reduce-scatter.34.cloned.1.call-done = bf16[256,1024]{0,1:T(8,128)(2,1)} async-done(((bf16[1024,1024]{0,1:T(8,128)(2,1)}), bf16[256,1024]{0,1:T(8,128)(2,1)}) %reduce-scatter.34.cloned.1.call-update) | async-done | bytes 524304 | tf_op jit(solution)/shard_map/reduce_scatter | solution.py:270
  1219.8 25.0 %reduce-scatter.36.cloned.1.call-done = bf16[64,2048]{1,0:T(8,128)(2,1)} async-done(((bf16[256,2048]{1,0:T(8,128)(2,1)}), bf16[64,2048]{1,0:T(8,128)(2,1)}) %reduce-scatter.36.cloned.1.call-update) | async-done | bytes 262160 | tf_op jit(solution)/shard_map/reduce_scatter | solution.py:301
  1255.8 15.8 all-gather.109.cloned.1.call-done
  1277.5 23.4 %all-gather.81.cloned.1.call-done = bf16[256,2048]{1,0:T(8,128)(2,1)} async-done(((bf16[64,2048]{1,0:T(8,128)(2,1)}), bf16[256,2048]{1,0:T(8,128)(2,1)}) %all-gather.81.cloned.1.call-update) | async-done | bytes 1048592 | tf_op jit(solution)/shard_map/all_gather | solution.py:219
  1348.1 25.4 %reduce-scatter.38.cloned.1.call-done = bf16[256,1024]{0,1:T(8,128)(2,1)} async-done(((bf16[1024,1024]{0,1:T(8,128)(2,1)}), bf16[256,1024]{0,1:T(8,128)(2,1)}) %reduce-scatter.38.cloned.1.call-update) | async-done | bytes 524304 | tf_op jit(solution)/shard_map/reduce_scatter | solution.py:270
  1402.5 25.0 %reduce-scatter.40.cloned.1.call-done = bf16[64,2048]{1,0:T(8,128)(2,1)} async-done(((bf16[256,2048]{1,0:T(8,128)(2,1)}), bf16[64,2048]{1,0:T(8,128)(2,1)}) %reduce-scatter.40.cloned.1.call-update) | async-done | bytes 262160 | tf_op jit(solution)/shard_map/reduce_scatter | solution.py:301
  1440.0 14.2 all-gather.113.cloned.1.call-done
  1460.5 23.3 %all-gather.83.cloned.1.call-done = bf16[256,2048]{1,0:T(8,128)(2,1)} async-done(((bf16[64,2048]{1,0:T(8,128)(2,1)}), bf16[256,2048]{1,0:T(8,128)(2,1)}) %all-gather.83.cloned.1.call-update) | async-done | bytes 1048592 | tf_op jit(solution)/shard_map/all_gather | solution.py:219
  1492.0 19.4 all-gather.115.cloned.1.call-done
  1580.5 15.2 fusion.526
  1595.8 13.7 fusion.527
  1619.7 13.6 fusion.525
  1643.6 15.6 fusion.524
  1661.5 26.5 %add_convert_fusion.1 = bf16[2560,2048]{1,0:T(8,128)(2,1)} fusion(f32[2560,2048]{1,0:T(8,128)} %fusion.191, f32[2560,2048]{1,0:T(8,128)} %fusion.193, f32[2560,2048]{1,0:T(8,128)} %fusion.195, f32[2560,2048]{1,0:T(8,128)} %fusion.197, bf16[256,2048]{1,0:T(8,128)(2,1)} %all-gather.83.cloned.1.call-done, pred[]{:T(512)S(6)} %and.120, pred[]{:T(512)S(6)} %and.118, ...), kind=kOutput, calls=%fused_computation.1 | convolution fusion | flops 2736783360 | bytes 96731144 | tf_op jit(solution)/shard_map/dot_general | solution.py:220
  1711.5 35.0 %add_convert_fusion = bf16[2048,3584]{1,0:T(8,128)(2,1)} fusion(f32[2048,3584]{1,0:T(8,128)} %fusion.524, f32[2048,3584]{1,0:T(8,128)} %fusion.525, f32[2048,3584]{1,0:T(8,128)} %fusion.526, f32[2048,3584]{1,0:T(8,128)} %fusion.527, bf16[256,2048]{1,0:T(8,128)(2,1)} %all-gather.93.cloned.1.call-done, pred[]{:T(512)S(6)} %and.120, pred[]{:T(512)S(6)} %and.118, ...), kind=kOutput, calls=%fused_computation | convolution fusion | flops 3838836736 | bytes 135004160 | tf_op jit(solution)/shard_map/dot_general | solution.py:295
  1758.1 16.3 all-reduce.1
  1775.6 19.8 all-reduce
  1796.9 407.8 %all-reduce.5.cloned.1.call-done = (bf16[2048,3584]{1,0:T(8,128)(2,1)}, bf16[2560,2048]{1,0:T(8,128)(2,1)}) async-done(((bf16[2048,3584]{1,0:T(8,128)(2,1)}, bf16[2560,2048]{1,0:T(8,128)(2,1)}), (bf16[2048,3584]{1,0:T(8,128)(2,1)}, bf16[2560,2048]{1,0:T(8,128)(2,1)})) %all-reduce.5.cloned.1.call-update) | async-done | bytes 25165840 | tf_op jit(solution)/shard_map/psum | solution.py:328
  2226.0 13.8 convert_element_type.735
  2244.5 12.6 copy.144
  2257.1 12.6 copy.150
  2269.7 21.2 slice_bitcast_fusion
  (889 shorter events, 916.8 us)
Async XLA Ops:
  12.8 67.7 %all-gather.49.cloned.1.call-start = ((), (), s32[]{:S(2)}) async-start(), calls=%async_computation.16 | async-start | bytes 1310720 | tf_op jit(solution)/shard_map/all_gather | solution.py:146
  54.6 54.7 %all-gather.51.cloned.1.call-start = ((), (), s32[]{:S(2)}) async-start(), calls=%async_computation.17 | async-start | bytes 1310720 | tf_op jit(solution)/shard_map/all_gather | solution.py:147
  59.1 92.4 %reduce-scatter.16.cloned.1.call-start = ((), (), s32[]{:S(2)}) async-start(), calls=%async_computation.18 | async-start | bytes 1310720 | tf_op jit(solution)/shard_map/reduce_scatter | solution.py:173
  124.0 60.7 %all-gather.53.cloned.1.call-start = ((), (), s32[]{:S(2)}) async-start(), calls=%async_computation.19 | async-start | bytes 1310720 | tf_op jit(solution)/shard_map/all_gather | solution.py:130
  156.7 72.6 %all-gather.55.cloned.1.call-start = ((), (), s32[]{:S(2)}) async-start(), calls=%async_computation.20 | async-start | bytes 1310720 | tf_op jit(solution)/shard_map/all_gather | solution.py:146
  203.4 54.1 %all-gather.57.cloned.1.call-start = ((), (), s32[]{:S(2)}) async-start(), calls=%async_computation.21 | async-start | bytes 1310720 | tf_op jit(solution)/shard_map/all_gather | solution.py:147
  210.9 90.9 %reduce-scatter.18.cloned.1.call-start = ((), (), s32[]{:S(2)}) async-start(), calls=%async_computation.22 | async-start | bytes 1310720 | tf_op jit(solution)/shard_map/reduce_scatter | solution.py:173
  274.4 61.5 %all-gather.59.cloned.1.call-start = ((), (), s32[]{:S(2)}) async-start(), calls=%async_computation.23 | async-start | bytes 1310720 | tf_op jit(solution)/shard_map/all_gather | solution.py:130
  307.9 72.6 %all-gather.61.cloned.1.call-start = ((), (), s32[]{:S(2)}) async-start(), calls=%async_computation.24 | async-start | bytes 1310720 | tf_op jit(solution)/shard_map/all_gather | solution.py:146
  354.6 54.2 %all-gather.63.cloned.1.call-start = ((), (), s32[]{:S(2)}) async-start(), calls=%async_computation.25 | async-start | bytes 1310720 | tf_op jit(solution)/shard_map/all_gather | solution.py:147
  358.2 94.8 %reduce-scatter.20.cloned.1.call-start = ((), (), s32[]{:S(2)}) async-start(), calls=%async_computation.26 | async-start | bytes 1310720 | tf_op jit(solution)/shard_map/reduce_scatter | solution.py:173
  425.6 61.5 %all-gather.65.cloned.1.call-start = ((), (), s32[]{:S(2)}) async-start(), calls=%async_computation.27 | async-start | bytes 1310720 | tf_op jit(solution)/shard_map/all_gather | solution.py:130
  459.1 72.5 %all-gather.67.cloned.1.call-start = ((), (), s32[]{:S(2)}) async-start(), calls=%async_computation.28 | async-start | bytes 1310720 | tf_op jit(solution)/shard_map/all_gather | solution.py:146
  509.4 79.8 %all-gather.97.cloned.1.call-start = ((), (), s32[]{:S(2)}) async-start(), calls=%async_computation.55 | async-start | bytes 1310720 | tf_op jit(solution)/shard_map/all_gather | solution.py:219
  511.7 106.8 %reduce-scatter.22.cloned.1.call-start = ((), (), s32[]{:S(2)}) async-start(), calls=%async_computation.30 | async-start | bytes 1310720 | tf_op jit(solution)/shard_map/reduce_scatter | solution.py:173
  576.7 75.9 %all-gather.71.cloned.1.call-start = ((), (), s32[]{:S(2)}) async-start(), calls=%async_computation.31 | async-start | bytes 1310720 | tf_op jit(solution)/shard_map/all_gather | solution.py:130
  625.6 85.4 %all-gather.73.cloned.1.call-start = ((), (), s32[]{:S(2)}) async-start(), calls=%async_computation.32 | async-start | bytes 1310720 | tf_op jit(solution)/shard_map/all_gather | solution.py:146
  685.2 68.3 %all-gather.95.cloned.1.call-start = ((), (), s32[]{:S(2)}) async-start(), calls=%async_computation.54 | async-start | bytes 1310720 | tf_op jit(solution)/shard_map/all_gather | solution.py:233
  697.6 84.1 %all-gather.99.cloned.1.call-start = ((), (), s32[]{:S(2)}) async-start(), calls=%async_computation.56 | async-start | bytes 1310720 | tf_op jit(solution)/shard_map/all_gather | solution.py:234
  709.0 117.8 %reduce-scatter.26.cloned.1.call-start = ((), (), s32[]{:S(2)}) async-start(), calls=%async_computation.35 | async-start | bytes 2621440 | tf_op jit(solution)/shard_map/reduce_scatter | solution.py:270
  791.4 88.6 %reduce-scatter.28.cloned.1.call-start = ((), (), s32[]{:S(2)}) async-start(), calls=%async_computation.36 | async-start | bytes 1310720 | tf_op jit(solution)/shard_map/reduce_scatter | solution.py:301
  852.6 54.2 %all-gather.101.cloned.1.call-start = ((), (), s32[]{:S(2)}) async-start(), calls=%async_computation.57 | async-start | bytes 1310720 | tf_op jit(solution)/shard_map/all_gather | solution.py:233
  853.3 82.9 %all-gather.77.cloned.1.call-start = ((), (), s32[]{:S(2)}) async-start(), calls=%async_computation.37 | async-start | bytes 1310720 | tf_op jit(solution)/shard_map/all_gather | solution.py:219
  891.3 72.3 %all-gather.103.cloned.1.call-start = ((), (), s32[]{:S(2)}) async-start(), calls=%async_computation.58 | async-start | bytes 1310720 | tf_op jit(solution)/shard_map/all_gather | solution.py:234
  891.9 116.8 %reduce-scatter.30.cloned.1.call-start = ((), (), s32[]{:S(2)}) async-start(), calls=%async_computation.38 | async-start | bytes 2621440 | tf_op jit(solution)/shard_map/reduce_scatter | solution.py:270
  973.3 88.6 %reduce-scatter.32.cloned.1.call-start = ((), (), s32[]{:S(2)}) async-start(), calls=%async_computation.39 | async-start | bytes 1310720 | tf_op jit(solution)/shard_map/reduce_scatter | solution.py:301
  1034.5 54.0 %all-gather.105.cloned.1.call-start = ((), (), s32[]{:S(2)}) async-start(), calls=%async_computation.59 | async-start | bytes 1310720 | tf_op jit(solution)/shard_map/all_gather | solution.py:233
  1035.1 83.0 %all-gather.79.cloned.1.call-start = ((), (), s32[]{:S(2)}) async-start(), calls=%async_computation.40 | async-start | bytes 1310720 | tf_op jit(solution)/shard_map/all_gather | solution.py:219
  1073.2 72.5 %all-gather.107.cloned.1.call-start = ((), (), s32[]{:S(2)}) async-start(), calls=%async_computation.60 | async-start | bytes 1310720 | tf_op jit(solution)/shard_map/all_gather | solution.py:234
  1074.0 116.9 %reduce-scatter.34.cloned.1.call-start = ((), (), s32[]{:S(2)}) async-start(), calls=%async_computation.41 | async-start | bytes 2621440 | tf_op jit(solution)/shard_map/reduce_scatter | solution.py:270
  1155.5 89.3 %reduce-scatter.36.cloned.1.call-start = ((), (), s32[]{:S(2)}) async-start(), calls=%async_computation.42 | async-start | bytes 1310720 | tf_op jit(solution)/shard_map/reduce_scatter | solution.py:301
  1217.3 54.2 %all-gather.109.cloned.1.call-start = ((), (), s32[]{:S(2)}) async-start(), calls=%async_computation.61 | async-start | bytes 1310720 | tf_op jit(solution)/shard_map/all_gather | solution.py:233
  1218.1 82.9 %all-gather.81.cloned.1.call-start = ((), (), s32[]{:S(2)}) async-start(), calls=%async_computation.43 | async-start | bytes 1310720 | tf_op jit(solution)/shard_map/all_gather | solution.py:219
  1254.6 73.8 %all-gather.111.cloned.1.call-start = ((), (), s32[]{:S(2)}) async-start(), calls=%async_computation.62 | async-start | bytes 1310720 | tf_op jit(solution)/shard_map/all_gather | solution.py:234
  1255.2 118.3 %reduce-scatter.38.cloned.1.call-start = ((), (), s32[]{:S(2)}) async-start(), calls=%async_computation.44 | async-start | bytes 2621440 | tf_op jit(solution)/shard_map/reduce_scatter | solution.py:270
  1338.2 89.3 %reduce-scatter.40.cloned.1.call-start = ((), (), s32[]{:S(2)}) async-start(), calls=%async_computation.45 | async-start | bytes 1310720 | tf_op jit(solution)/shard_map/reduce_scatter | solution.py:301
  1400.0 54.2 %all-gather.113.cloned.1.call-start = ((), (), s32[]{:S(2)}) async-start(), calls=%async_computation.63 | async-start | bytes 1310720 | tf_op jit(solution)/shard_map/all_gather | solution.py:233
  1400.7 83.0 %all-gather.83.cloned.1.call-start = ((), (), s32[]{:S(2)}) async-start(), calls=%async_computation.46 | async-start | bytes 1310720 | tf_op jit(solution)/shard_map/all_gather | solution.py:219
  1437.3 74.1 %all-gather.115.cloned.1.call-start = ((), (), s32[]{:S(2)}) async-start(), calls=%async_computation.64 | async-start | bytes 1310720 | tf_op jit(solution)/shard_map/all_gather | solution.py:234
  1438.0 142.5 %all-gather.87.cloned.1.call-start = ((), (), s32[]{:S(2)}) async-start(), calls=%async_computation.50 | async-start | bytes 1310720 | tf_op jit(solution)/shard_map/all_gather | solution.py:296
  1438.6 157.2 %all-gather.85.cloned.1.call-start = ((), (), s32[]{:S(2)}) async-start(), calls=%async_computation.49 | async-start | bytes 1310720 | tf_op jit(solution)/shard_map/all_gather | solution.py:296
  1439.3 180.3 %all-gather.89.cloned.1.call-start = ((), (), s32[]{:S(2)}) async-start(), calls=%async_computation.51 | async-start | bytes 1310720 | tf_op jit(solution)/shard_map/all_gather | solution.py:296
  1439.9 203.6 %all-gather.91.cloned.1.call-start = ((), (), s32[]{:S(2)}) async-start(), calls=%async_computation.52 | async-start | bytes 1310720 | tf_op jit(solution)/shard_map/all_gather | solution.py:296
  1460.2 231.3 %reduce-scatter.42.cloned.1.call-start = ((), (), s32[]{:S(2)}) async-start(), calls=%async_computation.47 | async-start | bytes 2621440 | tf_op jit(solution)/shard_map/reduce_scatter | solution.py:270
  1526.3 185.2 %all-gather.93.cloned.1.call-start = ((), (), s32[]{:S(2)}) async-start(), calls=%async_computation.53 | async-start | bytes 1310720 | tf_op jit(solution)/shard_map/all_gather | solution.py:296
  1544.1 204.9 %reduce-scatter.24.cloned.1.call-start = ((), (), s32[]{:S(2)}) async-start(), calls=%async_computation.34 | async-start | bytes 1310720 | tf_op jit(solution)/shard_map/reduce_scatter | solution.py:173
  1557.3 199.2 %reduce-scatter.44.cloned.1.call-start = ((), (), s32[]{:S(2)}) async-start(), calls=%async_computation.48 | async-start | bytes 1310720 | tf_op jit(solution)/shard_map/reduce_scatter | solution.py:301
  1711.4 493.2 %all-reduce.5.cloned.1.call-start = ((), (), s32[]{:S(2)}) async-start(), calls=%async_computation.65 | async-start | bytes 50331648 | tf_op jit(solution)/shard_map/psum | solution.py:328
  (193 other events, 8569.4 us)
Sparse Core Ops, SparseCore 0:
  13.0 30.6 all-gather.46
  54.7 25.7 all-gather.48
  82.9 26.3 all-gather.50
  124.1 27.2 reduce-scatter.15
  156.8 27.7 all-gather.52
  203.5 25.7 all-gather.54
  231.1 26.3 all-gather.56
  274.5 27.2 reduce-scatter.17
  308.0 27.7 all-gather.58
  354.7 25.7 all-gather.60
  382.3 26.3 all-gather.62
  425.7 27.2 reduce-scatter.19
  459.2 27.7 all-gather.64
  505.8 25.7 all-gather.66
  533.3 26.3 all-gather.68
  561.1 27.9 all-gather.96
  591.8 26.6 reduce-scatter.21
  625.7 26.8 all-gather.70
  671.4 25.7 all-gather.72
  698.9 26.3 all-gather.74
  727.1 26.3 all-gather.94
  755.3 26.3 all-gather.98
  791.5 35.1 reduce-scatter.25
  852.7 27.2 reduce-scatter.27
  908.2 27.9 all-gather.76
  937.9 25.7 all-gather.102
  973.4 35.1 reduce-scatter.29
  1034.6 27.2 reduce-scatter.31
  1090.1 27.9 all-gather.78
  1120.0 25.7 all-gather.106
  1155.6 35.1 reduce-scatter.33
  1217.5 27.2 reduce-scatter.35
  1272.9 27.9 all-gather.80
  1302.6 25.7 all-gather.110
  1338.3 35.1 reduce-scatter.37
  1400.1 27.2 reduce-scatter.39
  1429.3 24.8 all-gather.112
  1455.8 27.9 all-gather.82
  1485.6 25.7 all-gather.114
  1512.8 27.9 all-gather.86
  1542.4 27.3 all-gather.84
  1571.2 27.3 all-gather.88
  1600.0 27.3 all-gather.90
  1630.2 34.5 reduce-scatter.41
  1666.2 27.9 all-gather.92
  1696.4 26.6 reduce-scatter.23
  1726.0 25.7 reduce-scatter.43
  1756.0 448.6 all-reduce.4
  (3 shorter events, 74.4 us)
where the time goes:
time: 2310 us; the launch traced here: 2300 us
  waiting for transfers between devices  1210 us (52%)
  matrix products  482 us (21%)
  local copies, waits for them, and re-layouts  269 us (12%)
  other arithmetic  261 us (11%)
  blocking collectives  36.1 us (2%)
    psum x1, waiting for transfers between devices, on_device(): lax.psum(total_w_in.astype(jnp.bfloat16), 'ctx').astype(jnp.float32)  408 us
    all_gather x5, waiting for transfers between devices, on_device(): lax.all_gather(normed_b, 'tp', axis=0, tiled=True)  107 us
    reduce_scatter x5, waiting for transfers between devices, on_device(): lax.psum_scatter(lax.dot_general(grad_proj_b, w_in, contract_cols, prefer...  102 us
    reduce_scatter x5, waiting for transfers between devices, on_device(): lax.psum_scatter(jnp.dot(branch_in, w_out, preferred_element_type=jnp.flo...  101 us
    all_gather x5, waiting for transfers between devices, on_device(): fold_pieces = lax.all_gather(grad_out_b, 'tp', axis=0, tiled=True)  93.7 us
    dot_general x5, matrix products, on_device(): lax.dot_general(lax.all_gather(backward_normed_b, 'tp', axis=0, tiled=Tru...  93.2 us
    reduce_scatter x5, waiting for transfers between devices, on_device(): lax.psum_scatter(jnp.concatenate([grad_key_part, grad_value_part], axis=2...  86 us
    all_gather x5, waiting for transfers between devices, on_device(): values_part = lax.all_gather(values_b, 'ctx', axis=0, tiled=True)  85.2 us
  transfers between devices with their start and end apart: 59, of which 48 were waited for; matrix products, arithmetic and copies ran while one was open for 26% of the time, Pallas kernels for 0%

commit v1 on v0

--- a/solution.py
+++ b/solution.py
@@ -9,6 +9,19 @@
 NEGATIVE = -1e30
 GELU_ROOT = 0.7978845608028654
 GELU_CUBE = 0.044715
+
+
+def collect(array, axis, dim):
+    ways = lax.axis_size(axis)
+    up = [(d, (d + 1) % ways) for d in range(ways)]
+    down = [(d, (d - 1) % ways) for d in range(ways)]
+    earlier, later = ([array], [array])
+    for _ in range(ways // 2):
+        earlier.append(lax.ppermute(earlier[-1], axis, up))
+    for _ in range((ways - 1) // 2):
+        later.append(lax.ppermute(later[-1], axis, down))
+    line = jnp.concatenate([*earlier[::-1], *later[1:]], axis=dim)
+    return jnp.roll(line, (lax.axis_index(axis) - ways // 2) * array.shape[dim], axis=dim)
 
 
 def from_behind(x, axis, by):
@@ -216,7 +229,7 @@
         backward_doc_rows = lax.dynamic_slice_in_dim(doc_all, ctx_id * ctx_rows, ctx_rows)
         backward_branch_in = stored["branch_in"]
         grad_out_b = grad_out.astype(jnp.bfloat16)
-        fold_pieces = lax.all_gather(grad_out_b, "tp", axis=0, tiled=True)
+        fold_pieces = collect(grad_out_b, "tp", 0)
         grad_w = lax.dot_general(
             backward_branch_in, fold_pieces, contract_rows, preferred_element_type=jnp.float32
         )

time: 2310 us -> 2180 us (0.944)
  waiting for transfers between devices: 1210 us -> 1050 us
    all_gather x5 -> x0, waiting for transfers between devices: 93.7 us -> none  [on_device(): fold_pieces = lax.all_gather(grad_out_b, 'tp', axis=0, tiled=True)]
    ppermute x0 -> x15, waiting for transfers between devices: none -> 41.3 us  [the longest x10 37.6 us: collect(): earlier.append(lax.ppermute(earlier[-1], axis, up))]
    all_gather x5, waiting for transfers between devices: 79.8 us -> 41.9 us  [on_device(): keys_all = lax.all_gather(stored['keys'], 'ctx', axis=0, tiled=True)]
    all_gather x5, waiting for transfers between devices: 69.6 us -> 36 us  [on_device(): values_all = lax.all_gather(stored['values'], 'ctx', axis=0, tiled=True)]
    unnamed x367 -> x383, local copies, waits for them, and re-layouts: 64.8 us -> 66.9 us
  transfers between devices with their start and end apart: 59 -> 69, of which waited for: 48 -> 49; matrix products, arithmetic and copies ran while one was open for 26% -> 28% of each run, Pallas kernels for 0% -> 0%
where the time goes in v1:
time: 2180 us; the launch traced here: 2170 us
  waiting for transfers between devices  1050 us (48%)
  matrix products  484 us (22%)
  other arithmetic  278 us (13%)
  local copies, waits for them, and re-layouts  270 us (12%)
  starting transfers between devices  37.6 us (2%)
  blocking collectives  36.2 us (2%)
    psum x1, waiting for transfers between devices, on_device(): lax.psum(total_w_in.astype(jnp.bfloat16), 'ctx').astype(jnp.float32)  408 us
    all_gather x5, waiting for transfers between devices, on_device(): lax.all_gather(normed_b, 'tp', axis=0, tiled=True)  109 us
    reduce_scatter x5, waiting for transfers between devices, on_device(): lax.psum_scatter(lax.dot_general(grad_proj_b, w_in, contract_cols, prefer...  99.8 us
    dot_general x5, matrix products, on_device(): lax.dot_general(lax.all_gather(backward_normed_b, 'tp', axis=0, tiled=Tru...  96.7 us
    reduce_scatter x5, waiting for transfers between devices, on_device(): lax.psum_scatter(jnp.concatenate([grad_key_part, grad_value_part], axis=2...  86.2 us
    reduce_scatter x5, waiting for transfers between devices, on_device(): lax.psum_scatter(jnp.dot(branch_in, w_out, preferred_element_type=jnp.flo...  84.6 us
    all_gather x5, waiting for transfers between devices, on_device(): values_part = lax.all_gather(values_b, 'ctx', axis=0, tiled=True)  77.7 us
    dynamic_update_slice x49, other arithmetic, put_slot(): lax.dynamic_update_index_in_dim(buffer, jnp.where(active, leaf_value, tak...  71.3 us
  transfers between devices with their start and end apart: 69, of which 49 were waited for; matrix products, arithmetic and copies ran while one was open for 28% of the time, Pallas kernels for 0%

profile of v1, /device:TPU:0, one launch (start us, length us, event | category | flops | bytes accessed | tf_op | source)
XLA Modules:
  0.0 2170.5 jit_solution(10285569257207961900)
XLA Ops:
  19.1 12.1 pad_maximum_fusion
  31.2 12.5 all-gather.41.cloned.1.call-done
  61.7 18.8 all-gather.43.cloned.1.call-done
  89.4 19.9 all-gather.45.cloned.1.call-done
  124.1 27.4 %reduce-scatter.16.cloned.1.call-done = bf16[64,2048]{1,0:T(8,128)(2,1)} async-done(((bf16[256,2048]{1,0:T(8,128)(2,1)}), bf16[64,2048]{1,0:T(8,128)(2,1)}) %reduce-scatter.16.cloned.1.call-update) | async-done | bytes 262160 | tf_op jit(solution)/shard_map/reduce_scatter | solution.py:186
  156.8 27.9 %all-gather.47.cloned.1.call-done = bf16[256,2048]{1,0:T(8,128)(2,1)} async-done(((bf16[64,2048]{1,0:T(8,128)(2,1)}), bf16[256,2048]{1,0:T(8,128)(2,1)}) %all-gather.47.cloned.1.call-update) | async-done | bytes 1048592 | tf_op jit(solution)/shard_map/all_gather | solution.py:143
  216.0 13.3 all-gather.49.cloned.1.call-done
  238.3 19.2 all-gather.51.cloned.1.call-done
  275.1 26.7 %reduce-scatter.18.cloned.1.call-done = bf16[64,2048]{1,0:T(8,128)(2,1)} async-done(((bf16[256,2048]{1,0:T(8,128)(2,1)}), bf16[64,2048]{1,0:T(8,128)(2,1)}) %reduce-scatter.18.cloned.1.call-update) | async-done | bytes 262160 | tf_op jit(solution)/shard_map/reduce_scatter | solution.py:186
  308.1 27.7 %all-gather.53.cloned.1.call-done = bf16[256,2048]{1,0:T(8,128)(2,1)} async-done(((bf16[64,2048]{1,0:T(8,128)(2,1)}), bf16[256,2048]{1,0:T(8,128)(2,1)}) %all-gather.53.cloned.1.call-update) | async-done | bytes 1048592 | tf_op jit(solution)/shard_map/all_gather | solution.py:143
  363.1 17.4 all-gather.55.cloned.1.call-done
  389.6 19.2 all-gather.57.cloned.1.call-done
  426.4 26.7 %reduce-scatter.20.cloned.1.call-done = bf16[64,2048]{1,0:T(8,128)(2,1)} async-done(((bf16[256,2048]{1,0:T(8,128)(2,1)}), bf16[64,2048]{1,0:T(8,128)(2,1)}) %reduce-scatter.20.cloned.1.call-update) | async-done | bytes 262160 | tf_op jit(solution)/shard_map/reduce_scatter | solution.py:186
  459.6 27.5 %all-gather.59.cloned.1.call-done = bf16[256,2048]{1,0:T(8,128)(2,1)} async-done(((bf16[64,2048]{1,0:T(8,128)(2,1)}), bf16[256,2048]{1,0:T(8,128)(2,1)}) %all-gather.59.cloned.1.call-update) | async-done | bytes 1048592 | tf_op jit(solution)/shard_map/all_gather | solution.py:143
  551.1 11.1 all-gather.63.cloned.1.call-done
  627.6 13.0 all-gather.65.cloned.1.call-done
  720.9 20.7 all-gather.81.cloned.1.call-done
  750.6 19.2 all-gather.83.cloned.1.call-done
  804.6 10.2 reduce-scatter.26.cloned.1.call-done
  830.1 10.6 convolution_convert_fusion.4
  841.4 26.7 %reduce-scatter.28.cloned.1.call-done = bf16[64,2048]{1,0:T(8,128)(2,1)} async-done(((bf16[256,2048]{1,0:T(8,128)(2,1)}), bf16[64,2048]{1,0:T(8,128)(2,1)}) %reduce-scatter.28.cloned.1.call-update) | async-done | bytes 262160 | tf_op jit(solution)/shard_map/reduce_scatter | solution.py:314
  942.7 25.3 %reduce-scatter.30.cloned.1.call-done = bf16[256,1024]{0,1:T(8,128)(2,1)} async-done(((bf16[1024,1024]{0,1:T(8,128)(2,1)}), bf16[256,1024]{0,1:T(8,128)(2,1)}) %reduce-scatter.30.cloned.1.call-update) | async-done | bytes 524304 | tf_op jit(solution)/shard_map/reduce_scatter | solution.py:283
  983.2 10.6 convolution_convert_fusion.3
  996.4 24.9 %reduce-scatter.32.cloned.1.call-done = bf16[64,2048]{1,0:T(8,128)(2,1)} async-done(((bf16[256,2048]{1,0:T(8,128)(2,1)}), bf16[64,2048]{1,0:T(8,128)(2,1)}) %reduce-scatter.32.cloned.1.call-update) | async-done | bytes 262160 | tf_op jit(solution)/shard_map/reduce_scatter | solution.py:314
  1096.0 25.3 %reduce-scatter.34.cloned.1.call-done = bf16[256,1024]{0,1:T(8,128)(2,1)} async-done(((bf16[1024,1024]{0,1:T(8,128)(2,1)}), bf16[256,1024]{0,1:T(8,128)(2,1)}) %reduce-scatter.34.cloned.1.call-update) | async-done | bytes 524304 | tf_op jit(solution)/shard_map/reduce_scatter | solution.py:283
  1136.5 10.6 convolution_convert_fusion.2
  1148.9 25.7 %reduce-scatter.36.cloned.1.call-done = bf16[64,2048]{1,0:T(8,128)(2,1)} async-done(((bf16[256,2048]{1,0:T(8,128)(2,1)}), bf16[64,2048]{1,0:T(8,128)(2,1)}) %reduce-scatter.36.cloned.1.call-update) | async-done | bytes 262160 | tf_op jit(solution)/shard_map/reduce_scatter | solution.py:314
  1249.0 25.4 %reduce-scatter.38.cloned.1.call-done = bf16[256,1024]{0,1:T(8,128)(2,1)} async-done(((bf16[1024,1024]{0,1:T(8,128)(2,1)}), bf16[256,1024]{0,1:T(8,128)(2,1)}) %reduce-scatter.38.cloned.1.call-update) | async-done | bytes 524304 | tf_op jit(solution)/shard_map/reduce_scatter | solution.py:283
  1289.6 10.6 convolution_convert_fusion.1
  1305.2 22.5 %reduce-scatter.40.cloned.1.call-done = bf16[64,2048]{1,0:T(8,128)(2,1)} async-done(((bf16[256,2048]{1,0:T(8,128)(2,1)}), bf16[64,2048]{1,0:T(8,128)(2,1)}) %reduce-scatter.40.cloned.1.call-update) | async-done | bytes 262160 | tf_op jit(solution)/shard_map/reduce_scatter | solution.py:314
  1442.9 10.3 fusion.193
  1453.3 15.3 fusion.557
  1468.7 15.4 fusion.558
  1484.1 15.3 fusion.556
  1499.4 10.6 fusion.191
  1510.0 15.6 fusion.555
  1528.4 26.5 %add_convert_fusion.1 = bf16[2560,2048]{1,0:T(8,128)(2,1)} fusion(f32[2560,2048]{1,0:T(8,128)} %fusion.191, f32[2560,2048]{1,0:T(8,128)} %fusion.193, f32[2560,2048]{1,0:T(8,128)} %fusion.195, f32[2560,2048]{1,0:T(8,128)} %fusion.197, bf16[256,2048]{1,0:T(8,128)(2,1)S(1)} %copy-done.40, pred[]{:T(512)S(6)} %and.126, pred[]{:T(512)S(6)} %and.124, ...), kind=kOutput, calls=%fused_computation.1 | convolution fusion | flops 2736783360 | bytes 96731144 | tf_op jit(solution)/shard_map/dot_general | solution.py:233
  1573.7 10.3 convolution_convert_fusion
  1584.2 35.1 %add_convert_fusion = bf16[2048,3584]{1,0:T(8,128)(2,1)} fusion(f32[2048,3584]{1,0:T(8,128)} %fusion.555, f32[2048,3584]{1,0:T(8,128)} %fusion.556, f32[2048,3584]{1,0:T(8,128)} %fusion.557, f32[2048,3584]{1,0:T(8,128)} %fusion.558, bf16[256,2048]{1,0:T(8,128)(2,1)} %all-gather.79.cloned.1.call-done, pred[]{:T(512)S(6)} %and.126, pred[]{:T(512)S(6)} %and.124, ...), kind=kOutput, calls=%fused_computation | convolution fusion | flops 3838836736 | bytes 135004160 | tf_op jit(solution)/shard_map/dot_general | solution.py:308
  1630.7 16.2 all-reduce.1
  1648.1 20.0 all-reduce
  1669.6 407.9 %all-reduce.5.cloned.1.call-done = (bf16[2048,3584]{1,0:T(8,128)(2,1)}, bf16[2560,2048]{1,0:T(8,128)(2,1)}) async-done(((bf16[2048,3584]{1,0:T(8,128)(2,1)}, bf16[2560,2048]{1,0:T(8,128)(2,1)}), (bf16[2048,3584]{1,0:T(8,128)(2,1)}, bf16[2560,2048]{1,0:T(8,128)(2,1)})) %all-reduce.5.cloned.1.call-update) | async-done | bytes 25165840 | tf_op jit(solution)/shard_map/psum | solution.py:341
  2077.4 10.4 slice.551
  2087.9 10.8 convert_element_type.722
  2098.6 13.8 convert_element_type.735
  2117.1 12.6 copy.144
  2129.7 12.6 copy.150
  2142.3 21.2 slice_bitcast_fusion
  (925 shorter events, 884.3 us)
Async XLA Ops:
  7.2 36.5 %all-gather.41.cloned.1.call-start = ((), (), s32[]{:S(2)}) async-start(), calls=%async_computation.15 | async-start | bytes 1310720 | tf_op jit(solution)/shard_map/all_gather | solution.py:143
  12.8 67.7 %all-gather.43.cloned.1.call-start = ((), (), s32[]{:S(2)}) async-start(), calls=%async_computation.16 | async-start | bytes 1310720 | tf_op jit(solution)/shard_map/all_gather | solution.py:159
  54.6 54.7 %all-gather.45.cloned.1.call-start = ((), (), s32[]{:S(2)}) async-start(), calls=%async_computation.17 | async-start | bytes 1310720 | tf_op jit(solution)/shard_map/all_gather | solution.py:160
  59.1 92.4 %reduce-scatter.16.cloned.1.call-start = ((), (), s32[]{:S(2)}) async-start(), calls=%async_computation.18 | async-start | bytes 1310720 | tf_op jit(solution)/shard_map/reduce_scatter | solution.py:186
  124.0 60.6 %all-gather.47.cloned.1.call-start = ((), (), s32[]{:S(2)}) async-start(), calls=%async_computation.19 | async-start | bytes 1310720 | tf_op jit(solution)/shard_map/all_gather | solution.py:143
  156.7 72.6 %all-gather.49.cloned.1.call-start = ((), (), s32[]{:S(2)}) async-start(), calls=%async_computation.20 | async-start | bytes 1310720 | tf_op jit(solution)/shard_map/all_gather | solution.py:159
  203.4 54.1 %all-gather.51.cloned.1.call-start = ((), (), s32[]{:S(2)}) async-start(), calls=%async_computation.21 | async-start | bytes 1310720 | tf_op jit(solution)/shard_map/all_gather | solution.py:160
  211.1 90.7 %reduce-scatter.18.cloned.1.call-start = ((), (), s32[]{:S(2)}) async-start(), calls=%async_computation.22 | async-start | bytes 1310720 | tf_op jit(solution)/shard_map/reduce_scatter | solution.py:186
  274.3 61.5 %all-gather.53.cloned.1.call-start = ((), (), s32[]{:S(2)}) async-start(), calls=%async_computation.23 | async-start | bytes 1310720 | tf_op jit(solution)/shard_map/all_gather | solution.py:143
  307.9 72.6 %all-gather.55.cloned.1.call-start = ((), (), s32[]{:S(2)}) async-start(), calls=%async_computation.24 | async-start | bytes 1310720 | tf_op jit(solution)/shard_map/all_gather | solution.py:159
  354.6 54.2 %all-gather.57.cloned.1.call-start = ((), (), s32[]{:S(2)}) async-start(), calls=%async_computation.25 | async-start | bytes 1310720 | tf_op jit(solution)/shard_map/all_gather | solution.py:160
  358.2 94.8 %reduce-scatter.20.cloned.1.call-start = ((), (), s32[]{:S(2)}) async-start(), calls=%async_computation.26 | async-start | bytes 1310720 | tf_op jit(solution)/shard_map/reduce_scatter | solution.py:186
  425.6 61.5 %all-gather.59.cloned.1.call-start = ((), (), s32[]{:S(2)}) async-start(), calls=%async_computation.27 | async-start | bytes 1310720 | tf_op jit(solution)/shard_map/all_gather | solution.py:143
  459.1 82.8 %all-gather.61.cloned.1.call-start = ((), (), s32[]{:S(2)}) async-start(), calls=%async_computation.28 | async-start | bytes 1310720 | tf_op jit(solution)/shard_map/all_gather | solution.py:159
  505.7 56.4 %all-gather.63.cloned.1.call-start = ((), (), s32[]{:S(2)}) async-start(), calls=%async_computation.29 | async-start | bytes 1310720 | tf_op jit(solution)/shard_map/all_gather | solution.py:160
  537.1 69.3 %reduce-scatter.22.cloned.1.call-start = ((), (), s32[]{:S(2)}) async-start(), calls=%async_computation.30 | async-start | bytes 1310720 | tf_op jit(solution)/shard_map/reduce_scatter | solution.py:186
  579.0 61.6 %all-gather.65.cloned.1.call-start = ((), (), s32[]{:S(2)}) async-start(), calls=%async_computation.31 | async-start | bytes 1310720 | tf_op jit(solution)/shard_map/all_gather | solution.py:143
  613.6 85.2 %all-gather.67.cloned.1.call-start = ((), (), s32[]{:S(2)}) async-start(), calls=%async_computation.32 | async-start | bytes 1310720 | tf_op jit(solution)/shard_map/all_gather | solution.py:159
  659.4 54.2 %all-gather.69.cloned.1.call-start = ((), (), s32[]{:S(2)}) async-start(), calls=%async_computation.33 | async-start | bytes 1310720 | tf_op jit(solution)/shard_map/all_gather | solution.py:160
  673.3 68.4 %all-gather.81.cloned.1.call-start = ((), (), s32[]{:S(2)}) async-start(), calls=%async_computation.50 | async-start | bytes 1310720 | tf_op jit(solution)/shard_map/all_gather | solution.py:246
  685.7 84.2 %all-gather.83.cloned.1.call-start = ((), (), s32[]{:S(2)}) async-start(), calls=%async_computation.51 | async-start | bytes 1310720 | tf_op jit(solution)/shard_map/all_gather | solution.py:247
  697.1 117.8 %reduce-scatter.26.cloned.1.call-start = ((), (), s32[]{:S(2)}) async-start(), calls=%async_computation.35 | async-start | bytes 2621440 | tf_op jit(solution)/shard_map/reduce_scatter | solution.py:283
  779.5 88.6 %reduce-scatter.28.cloned.1.call-start = ((), (), s32[]{:S(2)}) async-start(), calls=%async_computation.36 | async-start | bytes 1310720 | tf_op jit(solution)/shard_map/reduce_scatter | solution.py:314
  840.7 54.0 %all-gather.85.cloned.1.call-start = ((), (), s32[]{:S(2)}) async-start(), calls=%async_computation.52 | async-start | bytes 1310720 | tf_op jit(solution)/shard_map/all_gather | solution.py:246
  841.4 81.6 %all-gather.87.cloned.1.call-start = ((), (), s32[]{:S(2)}) async-start(), calls=%async_computation.53 | async-start | bytes 1310720 | tf_op jit(solution)/shard_map/all_gather | solution.py:247
  878.8 89.2 %reduce-scatter.30.cloned.1.call-start = ((), (), s32[]{:S(2)}) async-start(), calls=%async_computation.37 | async-start | bytes 2621440 | tf_op jit(solution)/shard_map/reduce_scatter | solution.py:283
  932.6 88.6 %reduce-scatter.32.cloned.1.call-start = ((), (), s32[]{:S(2)}) async-start(), calls=%async_computation.38 | async-start | bytes 1310720 | tf_op jit(solution)/shard_map/reduce_scatter | solution.py:314
  993.8 54.2 %all-gather.89.cloned.1.call-start = ((), (), s32[]{:S(2)}) async-start(), calls=%async_computation.54 | async-start | bytes 1310720 | tf_op jit(solution)/shard_map/all_gather | solution.py:246
  994.6 81.6 %all-gather.91.cloned.1.call-start = ((), (), s32[]{:S(2)}) async-start(), calls=%async_computation.55 | async-start | bytes 1310720 | tf_op jit(solution)/shard_map/all_gather | solution.py:247
  1031.8 89.4 %reduce-scatter.34.cloned.1.call-start = ((), (), s32[]{:S(2)}) async-start(), calls=%async_computation.39 | async-start | bytes 2621440 | tf_op jit(solution)/shard_map/reduce_scatter | solution.py:283
  1031.9 22.3 %collective-permute-start.14 = (bf16[64,2048]{1,0:T(8,128)(2,1)S(1)}, bf16[64,2048]{1,0:T(8,128)(2,1)}, u32[]{:S(2)}, u32[]{:S(2)}) collective-permute-start(bf16[64,2048]{1,0:T(8,128)(2,1)S(1)} %get-tuple-element.66), channel_id=1, source_target_pairs={{0,3},{1,0},{2,1},{3,2},{4,7},{5,4},{6,5},{7,6},{8,11},{9,8},{10,9... | collective-permute-start | bytes 786440 | tf_op jit(solution)/shard_map/ppermute | solution.py:22
  1085.9 88.6 %reduce-scatter.36.cloned.1.call-start = ((), (), s32[]{:S(2)}) async-start(), calls=%async_computation.40 | async-start | bytes 1310720 | tf_op jit(solution)/shard_map/reduce_scatter | solution.py:314
  1147.1 54.2 %all-gather.93.cloned.1.call-start = ((), (), s32[]{:S(2)}) async-start(), calls=%async_computation.56 | async-start | bytes 1310720 | tf_op jit(solution)/shard_map/all_gather | solution.py:246
  1147.8 81.5 %all-gather.95.cloned.1.call-start = ((), (), s32[]{:S(2)}) async-start(), calls=%async_computation.57 | async-start | bytes 1310720 | tf_op jit(solution)/shard_map/all_gather | solution.py:247
  1183.6 90.7 %reduce-scatter.38.cloned.1.call-start = ((), (), s32[]{:S(2)}) async-start(), calls=%async_computation.41 | async-start | bytes 2621440 | tf_op jit(solution)/shard_map/reduce_scatter | solution.py:283
  1183.7 23.7 %collective-permute-start.18 = (bf16[64,2048]{1,0:T(8,128)(2,1)S(1)}, bf16[64,2048]{1,0:T(8,128)(2,1)}, u32[]{:S(2)}, u32[]{:S(2)}) collective-permute-start(bf16[64,2048]{1,0:T(8,128)(2,1)S(1)} %get-tuple-element.68), channel_id=1, source_target_pairs={{0,3},{1,0},{2,1},{3,2},{4,7},{5,4},{6,5},{7,6},{8,11},{9,8},{10,9... | collective-permute-start | bytes 786440 | tf_op jit(solution)/shard_map/ppermute | solution.py:22
  1239.0 88.7 %reduce-scatter.40.cloned.1.call-start = ((), (), s32[]{:S(2)}) async-start(), calls=%async_computation.42 | async-start | bytes 1310720 | tf_op jit(solution)/shard_map/reduce_scatter | solution.py:314
  1300.3 54.0 %all-gather.97.cloned.1.call-start = ((), (), s32[]{:S(2)}) async-start(), calls=%async_computation.58 | async-start | bytes 1310720 | tf_op jit(solution)/shard_map/all_gather | solution.py:246
  1300.8 81.5 %all-gather.99.cloned.1.call-start = ((), (), s32[]{:S(2)}) async-start(), calls=%async_computation.59 | async-start | bytes 1310720 | tf_op jit(solution)/shard_map/all_gather | solution.py:247
  1301.4 151.9 %all-gather.73.cloned.1.call-start = ((), (), s32[]{:S(2)}) async-start(), calls=%async_computation.46 | async-start | bytes 1310720 | tf_op jit(solution)/shard_map/all_gather | solution.py:309
  1302.2 166.5 %all-gather.71.cloned.1.call-start = ((), (), s32[]{:S(2)}) async-start(), calls=%async_computation.45 | async-start | bytes 1310720 | tf_op jit(solution)/shard_map/all_gather | solution.py:309
  1302.8 181.3 %all-gather.75.cloned.1.call-start = ((), (), s32[]{:S(2)}) async-start(), calls=%async_computation.47 | async-start | bytes 1310720 | tf_op jit(solution)/shard_map/all_gather | solution.py:309
  1303.5 206.5 %all-gather.77.cloned.1.call-start = ((), (), s32[]{:S(2)}) async-start(), calls=%async_computation.48 | async-start | bytes 1310720 | tf_op jit(solution)/shard_map/all_gather | solution.py:309
  1360.3 198.2 %reduce-scatter.42.cloned.1.call-start = ((), (), s32[]{:S(2)}) async-start(), calls=%async_computation.43 | async-start | bytes 2621440 | tf_op jit(solution)/shard_map/reduce_scatter | solution.py:283
  1397.1 187.0 %all-gather.79.cloned.1.call-start = ((), (), s32[]{:S(2)}) async-start(), calls=%async_computation.49 | async-start | bytes 1310720 | tf_op jit(solution)/shard_map/all_gather | solution.py:309
  1419.8 201.8 %reduce-scatter.24.cloned.1.call-start = ((), (), s32[]{:S(2)}) async-start(), calls=%async_computation.34 | async-start | bytes 1310720 | tf_op jit(solution)/shard_map/reduce_scatter | solution.py:186
  1432.8 196.4 %reduce-scatter.44.cloned.1.call-start = ((), (), s32[]{:S(2)}) async-start(), calls=%async_computation.44 | async-start | bytes 1310720 | tf_op jit(solution)/shard_map/reduce_scatter | solution.py:314
  1584.1 493.4 %all-reduce.5.cloned.1.call-start = ((), (), s32[]{:S(2)}) async-start(), calls=%async_computation.60 | async-start | bytes 50331648 | tf_op jit(solution)/shard_map/psum | solution.py:341
  (211 other events, 7661.9 us)
Sparse Core Ops, SparseCore 0:
  13.0 30.6 all-gather.40
  54.7 25.7 all-gather.42
  82.9 26.3 all-gather.44
  124.1 27.2 reduce-scatter.15
  156.8 27.7 all-gather.46
  203.5 25.7 all-gather.48
  231.1 26.3 all-gather.50
  274.5 27.2 reduce-scatter.17
  308.0 27.7 all-gather.52
  354.7 25.7 all-gather.54
  382.3 26.3 all-gather.56
  425.7 27.2 reduce-scatter.19
  459.3 27.7 all-gather.58
  505.9 25.7 all-gather.60
  537.2 24.9 all-gather.62
  579.1 27.2 reduce-scatter.21
  613.8 26.7 all-gather.64
  659.5 25.7 all-gather.66
  687.1 26.4 all-gather.68
  715.2 26.3 all-gather.80
  743.5 26.3 all-gather.82
  779.7 35.1 reduce-scatter.25
  840.8 27.2 reduce-scatter.27
  869.8 24.8 all-gather.84
  896.6 26.3 all-gather.86
  932.8 35.1 reduce-scatter.29
  994.0 27.2 reduce-scatter.31
  1023.1 24.8 all-gather.88
  1049.8 26.3 all-gather.90
  1086.0 35.1 reduce-scatter.33
  1147.2 27.2 reduce-scatter.35
  1176.4 24.8 all-gather.92
  1203.0 26.3 all-gather.94
  1239.2 35.1 reduce-scatter.37
  1300.4 27.2 reduce-scatter.39
  1329.4 24.8 all-gather.96
  1355.9 26.3 all-gather.98
  1383.9 27.9 all-gather.72
  1413.3 27.3 all-gather.70
  1442.3 27.3 all-gather.74
  1471.3 27.3 all-gather.76
  1501.6 34.5 reduce-scatter.41
  1537.7 27.9 all-gather.78
  1568.0 26.6 reduce-scatter.23
  1597.4 25.7 reduce-scatter.43
  1627.4 450.0 all-reduce.4
